TPU v7x, 32 devices: a whole 2x2x4 slice. The times are simulated.
32 devices in a mesh: expert: 8 (over z, y), dp: 4 (over x, core).
Axes of the slice: x: 2, y: 2, z: 4, core: 2. Of those that a mesh axis runs over, the one named last changes fastest.
Arguments:
- tokens: bfloat16 [4096, 1664], P(('expert', 'dp')), may hold values from -6 to 6
- out_grad: bfloat16 [4096, 1664], P(('expert', 'dp')), may hold values from -6 to 6
- expert_index: int32 [4096, 2], P(('expert', 'dp')), may hold values from 0 to 7, as said below
- slots: int32 [4096, 2], P(('expert', 'dp')), may hold values from -1 to 23, as said below
- combine: bfloat16 [4096, 2], P(('expert', 'dp')), may hold values from 0.099609375 to 1
- w_in: bfloat16 [8, 1664, 4096], P('expert', None, 'dp'), may hold values from -0.15625 to 0.15625
- b_in: float32 [8, 4096], P('expert', 'dp'), may hold values from -3 to 3
- w_out: bfloat16 [8, 4096, 1664], P('expert', 'dp'), may hold values from -0.09375 to 0.09375
Outputs:
- d_tokens: bfloat16 [4096, 1664], P(('expert', 'dp'))
- grad_w_in: float32 [8, 1664, 4096], P('expert', None, 'dp')
- grad_w_out: float32 [8, 4096, 1664], P('expert', 'dp')
- grad_b_in: float32 [8, 4096], P('expert', 'dp')
Inputs may be any that keep to these rules, and one draw needn't show every extreme that they name: `expert_index`: the two experts of a token differ. `slots`: a slot counts the earlier assignments to the same expert among the tokens of the same device, all first choices in token order before all second choices; it is -1 where that count reaches 24 (the assignment is dropped). So an expert takes at most 24 rows from one device, and in every draw some expert takes exactly 24 rows from every device.
All inputs are finite; a program needn't handle non-finite values.
Results may differ from a plain program's by a relative error of at most 0.01.
Values may be sent and summed in bfloat16 or wider, within the bound.
No kernel may reach another device: no remote copies, remote signals or barrier semaphores. Data moves between devices by JAX's collectives and lax.ppermute only.
A program may use at most 128 MiB of HBM per device.

v0:
```python
import jax
import jax.numpy as jnp
from jax import lax
from jax.sharding import PartitionSpec as P

inv_root_two = 0.7071067811865476
inv_root_two_pi = 0.3989422804014327


def gelu_value(values):
    return 0.5 * values * (1.0 + lax.erf(values * inv_root_two))


def gelu_slope(values):
    normal_cdf = 0.5 * (1.0 + lax.erf(values * inv_root_two))
    density = jnp.exp(-0.5 * values * values) * inv_root_two_pi
    return normal_cdf + values * density


def select(chosen, places, expert_count, capacity):
    expert_ids = jnp.arange(expert_count, dtype=jnp.int32)[:, None, None]
    slot_ids = jnp.arange(capacity, dtype=jnp.int32)[None, :, None]
    picks = []
    for member in range(2):
        same_expert = jnp.expand_dims(chosen[..., member], (-3, -2)) == expert_ids
        same_slot = jnp.expand_dims(places[..., member], (-3, -2)) == slot_ids
        picks.append((same_expert & same_slot).astype(jnp.bfloat16))
    return (picks[0], picks[1])


def scaled(weights, grads):
    grad_wide = grads.astype(jnp.float32)
    scaled_first = (weights[..., 0:1].astype(jnp.float32) * grad_wide).astype(jnp.bfloat16)
    scaled_second = (weights[..., 1:2].astype(jnp.float32) * grad_wide).astype(jnp.bfloat16)
    return (scaled_first, scaled_second)


def dispatch(inputs, scaled_first, scaled_second, pick_first, pick_second):
    rows_x = jnp.einsum(
        "recn,rnd->recd", pick_first + pick_second, inputs, preferred_element_type=jnp.float32
    )
    rows_g = jnp.einsum(
        "recn,rnd->recd", pick_first, scaled_first, preferred_element_type=jnp.float32
    )
    rows_g = rows_g + jnp.einsum(
        "recn,rnd->recd", pick_second, scaled_second, preferred_element_type=jnp.float32
    )
    return (rows_x.astype(jnp.bfloat16), rows_g.astype(jnp.bfloat16))


def on_device(tokens, out_grad, expert_index, slots, combine, w_in, b_in, w_out):
    expert_count = lax.axis_size("expert")
    replica_count = lax.axis_size("dp")
    tok_count, feat_width = tokens.shape
    capacity = max(2, (3 * tok_count + 2 * expert_count - 1) // (2 * expert_count))
    own_first, own_second = select(expert_index, slots, expert_count, capacity)
    pooled = (
        lax.all_gather(tokens, "dp", axis=0, tiled=True),
        lax.all_gather(out_grad, "dp", axis=0, tiled=True),
        lax.all_gather(combine, "dp", axis=0, tiled=True),
        lax.all_gather(expert_index, "dp", axis=0, tiled=True),
        lax.all_gather(slots, "dp", axis=0, tiled=True),
    )
    shaped = [array.reshape((replica_count, tok_count) + array.shape[1:]) for array in pooled]
    tok_all, grad_all, weight_all, chosen_all, places_all = shaped
    pick_first, pick_second = select(chosen_all, places_all, expert_count, capacity)
    scaled_first, scaled_second = scaled(weight_all, grad_all)
    send_x, send_g = dispatch(tok_all, scaled_first, scaled_second, pick_first, pick_second)
    rows_x, rows_g = (
        lax.all_to_all(send_x, "expert", split_axis=1, concat_axis=1, tiled=True),
        lax.all_to_all(send_g, "expert", split_axis=1, concat_axis=1, tiled=True),
    )
    rows_x = rows_x.reshape(-1, feat_width)
    rows_g = rows_g.reshape(-1, feat_width)
    first_w = w_in[0]
    second_w = w_out[0]
    pre_act = jnp.dot(rows_x, first_w, preferred_element_type=jnp.float32) + b_in[0]
    hidden = gelu_value(pre_act).astype(jnp.bfloat16)
    grad_second = lax.dot_general(
        hidden, rows_g, (((0,), (0,)), ((), ())), preferred_element_type=jnp.float32
    )
    d_hidden = lax.dot_general(
        rows_g, second_w, (((1,), (1,)), ((), ())), preferred_element_type=jnp.float32
    )
    d_pre = (d_hidden * gelu_slope(pre_act)).astype(jnp.bfloat16)
    grad_bias = jnp.sum(d_pre.astype(jnp.float32), axis=0)
    grad_first = lax.dot_general(
        rows_x, d_pre, (((0,), (0,)), ((), ())), preferred_element_type=jnp.float32
    )
    term = lax.dot_general(
        d_pre, first_w, (((1,), (1,)), ((), ())), preferred_element_type=jnp.float32
    )
    summed = lax.psum_scatter(
        lax.optimization_barrier(term.astype(jnp.bfloat16))
        .astype(jnp.float32)
        .astype(jnp.bfloat16),
        "dp",
        scatter_dimension=0,
        tiled=True,
    )
    d_rows = summed.reshape(expert_count, capacity, feat_width)
    returned = lax.all_to_all(d_rows, "expert", split_axis=0, concat_axis=0, tiled=True)
    d_tokens = jnp.einsum(
        "ecn,ecd->nd", own_first + own_second, returned, preferred_element_type=jnp.float32
    )
    return (d_tokens.astype(jnp.bfloat16), grad_first[None], grad_second[None], grad_bias[None])


def solution(mesh):
    in_specs = (
        P(("expert", "dp"), None),
        P(("expert", "dp"), None),
        P(("expert", "dp"), None),
        P(("expert", "dp"), None),
        P(("expert", "dp"), None),
        P("expert", None, "dp"),
        P("expert", "dp"),
        P("expert", "dp", None),
    )
    out_specs = (
        P(("expert", "dp"), None),
        P("expert", None, "dp"),
        P("expert", "dp", None),
        P("expert", "dp"),
    )
    return jax.shard_map(
        on_device, mesh=mesh, in_specs=in_specs, out_specs=out_specs, check_vma=False
    )
```

profile of v0, /device:TPU:0, one launch (start us, length us, event | category | flops | bytes accessed | tf_op | source)
XLA Modules:
  0.0 241.4 jit_solution(12847972751071568770)
XLA Ops:
  7.2 0.0 copy-start
  7.2 0.0 all-gather.5.cloned.1.call-start
  7.2 0.7 all-gather.5.cloned.1.call-update
  7.9 6.4 %all_gather.15 = s32[512,2]{0,1:T(2,128)S(1)} all-gather(s32[128,2]{0,1:T(2,128)} %param.10), channel_id=1, replica_groups=mesh['expert'=8,'dp'=4] {'dp'}, dimensions={0}, use_global_device_ids=true | all-gather | bytes 5120 | tf_op jit(solution)/shard_map/all_gather | solution.py:61
  14.3 5.5 %all_gather.16 = s32[512,2]{0,1:T(2,128)S(1)} all-gather(s32[128,2]{0,1:T(2,128)} %param.11), channel_id=1, replica_groups=mesh['expert'=8,'dp'=4] {'dp'}, dimensions={0}, use_global_device_ids=true | all-gather | bytes 5120 | tf_op jit(solution)/shard_map/all_gather | solution.py:62
  19.9 12.8 %all-gather.5.cloned.1.call-done = bf16[512,1664]{1,0:T(8,128)(2,1)} async-done(((bf16[128,1664]{1,0:T(8,128)(2,1)}), bf16[512,1664]{1,0:T(8,128)(2,1)}) %all-gather.5.cloned.1.call-update) | async-done | bytes 1703952 | tf_op jit(solution)/shard_map/all_gather | solution.py:58
  32.7 2.3 convolution_convert_fusion
  35.0 1.7 copy.16
  36.7 0.0 copy-start.7
  36.7 5.6 %all-to-all-start.1 = ((bf16[4,8,24,1664]{3,2,0,1:T(8,128)(2,1)}), bf16[4,8,24,1664]{3,2,0,1:T(8,128)(2,1)}, u32[]{:S(2)}, u32[]{:S(2)}) async-start(bf16[4,8,24,1664]{3,2,0,1:T(8,128)(2,1)} %copy.16), calls=%async_computation.1 | async-start | bytes 5111808 | tf_op jit(solution)/shard_map/all_to_all | solution.py:70
  42.3 0.0 all-gather.3.cloned.1.call-start
  42.4 0.7 all-gather.3.cloned.1.call-update
  43.1 0.0 copy-done.7
  43.1 5.0 %all_gather.17 = bf16[512,2]{0,1:T(2,128)(2,1)S(1)} all-gather(bf16[128,2]{0,1:T(2,128)(2,1)S(1)} %copy-done.7), channel_id=1, replica_groups=mesh['expert'=8,'dp'=4] {'dp'}, dimensions={0}, use_global_device_ids=true | all-gather | bytes 2560 | tf_op jit(solution)/shard_map/all_gather | solution.py:60
  48.1 17.5 %all-gather.3.cloned.1.call-done = bf16[512,1664]{1,0:T(8,128)(2,1)} async-done(((bf16[128,1664]{1,0:T(8,128)(2,1)}), bf16[512,1664]{1,0:T(8,128)(2,1)}) %all-gather.3.cloned.1.call-update) | async-done | bytes 1703952 | tf_op jit(solution)/shard_map/all_gather | solution.py:59
  65.6 2.5 %fusion.23 = f32[4,8,24,1664]{3,2,1,0:T(8,128)S(1)} fusion(bf16[4,128,1664]{2,1,0:T(8,128)(2,1)} %bitcast.84, f32[4,128]{1,0:T(4,128)S(1)} %get-tuple-element.9, pred[4,24,128]{2,1,0:T(8,128)(4,1)S(1)} %iota_compare_fusion.1, pred[4,8,128]{2,1,0:T(8,128)(4,1)S(1)} %iota_compare_fusion.3), kind=kOutput, calls=%fused_computation.29 | convolution fusion | flops 329809920 | bytes 6834176 | tf_op jit(solution)/shard_map/recn,rnd->recd/dot_general | solution.py:42
  68.1 0.0 copy-done.1
  68.1 0.9 add_convert_fusion
  69.0 1.7 copy.14
  70.7 30.2 %all-to-all-done.1 = bf16[4,8,24,1664]{3,2,0,1:T(8,128)(2,1)} async-done(((bf16[4,8,24,1664]{3,2,0,1:T(8,128)(2,1)}), bf16[4,8,24,1664]{3,2,0,1:T(8,128)(2,1)}, u32[]{:S(2)}, u32[]{:S(2)}) %all-to-all-start.1) | async-done | bytes 2555936 | tf_op jit(solution)/shard_map/all_to_all | solution.py:70
  100.9 4.4 %all-to-all-start = ((bf16[4,8,24,1664]{3,2,0,1:T(8,128)(2,1)}), bf16[4,8,24,1664]{3,2,0,1:T(8,128)(2,1)}, u32[]{:S(2)}, u32[]{:S(2)}) async-start(bf16[4,8,24,1664]{3,2,0,1:T(8,128)(2,1)} %copy.14), calls=%async_computation | async-start | bytes 5111808 | tf_op jit(solution)/shard_map/all_to_all | solution.py:71
  105.3 0.0 reduce-scatter.2.cloned.1.call-start
  105.4 1.9 copy.17
  107.3 0.0 copy-start.2
  107.3 1.5 copy-done.2
  108.8 0.0 copy-done
  108.8 4.7 %fusion.4 = f32[768,1024]{1,0:T(8,128)} fusion(bf16[768,1664]{1,0:T(8,128)(2,1)S(1)} %bitcast.87, bf16[1,1664,1024]{2,1,0:T(8,128)(2,1)S(1)} %copy-done), kind=kOutput, calls=%fused_computation.10 | convolution fusion | flops 2617245696 | bytes 9109504 | tf_op jit(solution)/shard_map/dot_general | solution.py:77
  113.5 49.5 %all-to-all-done = bf16[4,8,24,1664]{3,2,0,1:T(8,128)(2,1)} async-done(((bf16[4,8,24,1664]{3,2,0,1:T(8,128)(2,1)}), bf16[4,8,24,1664]{3,2,0,1:T(8,128)(2,1)}, u32[]{:S(2)}, u32[]{:S(2)}) %all-to-all-start) | async-done | bytes 2555936 | tf_op jit(solution)/shard_map/all_to_all | solution.py:71
  163.0 2.1 copy.15
  165.1 0.0 copy-start.3
  165.1 0.0 copy-done.9
  165.1 0.6 copy-done.8
  165.7 6.4 %convert_reduce_fusion = (f32[1024]{0:T(1024)}, bf16[768,1024]{1,0:T(8,128)(2,1)S(1)}) fusion(f32[768,1024]{1,0:T(8,128)} %fusion.4, f32[1024]{0:T(1024)S(1)} %bitcast.92, bf16[768,1664]{1,0:T(8,128)(2,1)S(1)} %bitcast.89, bf16[1,1024,1664]{2,1,0:T(8,128)(2,1)S(1)} %copy-done.8), kind=kOutput, calls=%fused_computation.22 | convolution fusion | flops 2627468288 | bytes 10690560 | tf_op jit(solution)/shard_map/dot_general | solution.py:82
  172.1 0.0 copy-done.3
  172.2 1.1 copy-done.11
  173.3 4.3 %fusion.8 = bf16[768,1664]{1,0:T(8,128)(2,1)} fusion(bf16[768,1024]{1,0:T(8,128)(2,1)S(1)} %get-tuple-element.15, bf16[1,1664,1024]{2,1,0:T(8,128)(2,1)S(1)} %copy-done), kind=kOutput, calls=%fused_computation.14 | convolution fusion | flops 2618523648 | bytes 7536640 | tf_op jit(solution)/shard_map/dot_general | solution.py:90
  177.6 0.0 reduce-scatter.2.cloned.1.call-update
  177.7 0.0 copy-done.5
  177.7 0.0 copy-done.6
  177.7 32.4 %reduce-scatter.2.cloned.1.call-done = bf16[192,1664]{1,0:T(8,128)(2,1)} async-done(((bf16[768,1664]{1,0:T(8,128)(2,1)}), bf16[192,1664]{1,0:T(8,128)(2,1)}) %reduce-scatter.2.cloned.1.call-update) | async-done | bytes 638992 | tf_op jit(solution)/shard_map/reduce_scatter | solution.py:93
  210.2 5.5 %all-to-all-start.2 = ((bf16[8,24,1664]{2,1,0:T(8,128)(2,1)}), bf16[8,24,1664]{2,1,0:T(8,128)(2,1)}, u32[]{:S(2)}, u32[]{:S(2)}) async-start(bf16[8,24,1664]{2,1,0:T(8,128)(2,1)} %bitcast.91), calls=%async_computation.3 | async-start | bytes 1277952 | tf_op jit(solution)/shard_map/all_to_all | solution.py:102
  215.7 0.0 copy-start.10
  215.7 8.1 %convolution_bitcast_fusion.1 = f32[1,1664,1024]{2,1,0:T(8,128)} fusion(bf16[768,1664]{1,0:T(8,128)(2,1)} %bitcast.88, bf16[768,1024]{1,0:T(8,128)(2,1)} %copy-done.11), kind=kOutput, calls=%fused_computation.3 | convolution fusion | flops 2617245696 | bytes 10944512 | tf_op jit(solution)/shard_map/dot_general | solution.py:87
  223.8 0.0 copy-done.4
  223.8 0.0 copy-done.10
  223.8 5.1 %convolution_bitcast_fusion = f32[1,1024,1664]{2,1,0:T(8,128)} fusion(bf16[768,1664]{1,0:T(8,128)(2,1)S(1)} %bitcast.90, f32[768,1024]{1,0:T(8,128)S(1)} %copy-done.10, f32[1024]{0:T(1024)S(1)} %bitcast.93), kind=kOutput, calls=%fused_computation.2 | convolution fusion | flops 2621964288 | bytes 12521472 | tf_op jit(solution)/shard_map/dot_general | solution.py:79
  228.9 3.9 %all-to-all-done.2 = bf16[8,24,1664]{2,1,0:T(8,128)(2,1)} async-done(((bf16[8,24,1664]{2,1,0:T(8,128)(2,1)}), bf16[8,24,1664]{2,1,0:T(8,128)(2,1)}, u32[]{:S(2)}, u32[]{:S(2)}) %all-to-all-start.2) | async-done | bytes 639008 | tf_op jit(solution)/shard_map/all_to_all | solution.py:102
  232.7 2.2 fusion.17
  (21 shorter events, 0.1 us)
Async XLA Ops:
  7.2 101.6 %copy-start = (bf16[1,1664,1024]{2,1,0:T(8,128)(2,1)S(1)}, bf16[1,1664,1024]{2,1,0:T(8,128)(2,1)}, u32[]{:S(2)}) copy-start(bf16[1,1664,1024]{2,1,0:T(8,128)(2,1)} %param.13) | copy-start | bytes 10223620
  7.2 25.5 %all-gather.5.cloned.1.call-start = ((), (), s32[]{:S(2)}) async-start(), calls=%async_computation.5 | async-start | bytes 2129920 | tf_op jit(solution)/shard_map/all_gather | solution.py:58
  36.7 6.4 %copy-start.7 = (bf16[128,2]{0,1:T(2,128)(2,1)S(1)}, bf16[128,2]{0,1:T(2,128)(2,1)}, u32[]{:S(2)}) copy-start(bf16[128,2]{0,1:T(2,128)(2,1)} %param.12) | copy-start | bytes 1540
  36.7 64.2 %all-to-all-start.1 = ((bf16[4,8,24,1664]{3,2,0,1:T(8,128)(2,1)}), bf16[4,8,24,1664]{3,2,0,1:T(8,128)(2,1)}, u32[]{:S(2)}, u32[]{:S(2)}) async-start(bf16[4,8,24,1664]{3,2,0,1:T(8,128)(2,1)} %copy.16), calls=%async_computation.1 | async-start | bytes 5111808 | tf_op jit(solution)/shard_map/all_to_all | solution.py:70
  42.3 23.3 %all-gather.3.cloned.1.call-start = ((), (), s32[]{:S(2)}) async-start(), calls=%async_computation.4 | async-start | bytes 2129920 | tf_op jit(solution)/shard_map/all_gather | solution.py:59
  65.6 2.5 %copy-start.1 = (bf16[512,1664]{1,0:T(8,128)(2,1)S(1)}, bf16[512,1664]{1,0:T(8,128)(2,1)}, u32[]{:S(2)}) copy-start(bf16[512,1664]{1,0:T(8,128)(2,1)} %all-gather.3.cloned.1.call-done) | copy-start | bytes 5111812
  100.9 62.1 %all-to-all-start = ((bf16[4,8,24,1664]{3,2,0,1:T(8,128)(2,1)}), bf16[4,8,24,1664]{3,2,0,1:T(8,128)(2,1)}, u32[]{:S(2)}, u32[]{:S(2)}) async-start(bf16[4,8,24,1664]{3,2,0,1:T(8,128)(2,1)} %copy.14), calls=%async_computation | async-start | bytes 5111808 | tf_op jit(solution)/shard_map/all_to_all | solution.py:71
  105.3 104.8 %reduce-scatter.2.cloned.1.call-start = ((), (), s32[]{:S(2)}) async-start(), calls=%async_computation.6 | async-start | bytes 3194880 | tf_op jit(solution)/shard_map/reduce_scatter | solution.py:93
  107.3 1.5 copy-start.2
  113.5 51.6 %copy-start.9 = (f32[1,1024]{1,0:T(1,128)S(1)}, f32[1,1024]{1,0:T(1,128)}, u32[]{:S(2)}) copy-start(f32[1,1024]{1,0:T(1,128)} %param.14) | copy-start | bytes 12292
  163.0 2.7 %copy-start.8 = (bf16[1,1024,1664]{2,1,0:T(8,128)(2,1)S(1)}, bf16[1,1024,1664]{2,1,0:T(8,128)(2,1)}, u32[]{:S(2)}) copy-start(bf16[1,1024,1664]{2,1,0:T(8,128)(2,1)} %param.15) | copy-start | bytes 10223620
  165.1 7.1 %copy-start.3 = (bf16[4,8,24,1664]{3,2,1,0:T(8,128)(2,1)}, bf16[4,8,24,1664]{3,2,1,0:T(8,128)(2,1)S(1)}, u32[]{:S(2)}) copy-start(bf16[4,8,24,1664]{3,2,1,0:T(8,128)(2,1)S(1)} %copy.15) | copy-start | bytes 7667716
  172.2 1.2 copy-start.11
  173.3 4.4 %copy-start.5 = (s32[128,2]{0,1:T(2,128)S(1)}, s32[128,2]{0,1:T(2,128)}, u32[]{:S(2)}) copy-start(s32[128,2]{0,1:T(2,128)} %param.10) | copy-start | bytes 3076
  173.3 4.4 %copy-start.6 = (s32[128,2]{0,1:T(2,128)S(1)}, s32[128,2]{0,1:T(2,128)}, u32[]{:S(2)}) copy-start(s32[128,2]{0,1:T(2,128)} %param.11) | copy-start | bytes 3076
  210.2 22.6 %all-to-all-start.2 = ((bf16[8,24,1664]{2,1,0:T(8,128)(2,1)}), bf16[8,24,1664]{2,1,0:T(8,128)(2,1)}, u32[]{:S(2)}, u32[]{:S(2)}) async-start(bf16[8,24,1664]{2,1,0:T(8,128)(2,1)} %bitcast.91), calls=%async_computation.3 | async-start | bytes 1277952 | tf_op jit(solution)/shard_map/all_to_all | solution.py:102
  215.7 8.1 %copy-start.4 = (bf16[4,8,24,1664]{3,2,1,0:T(8,128)(2,1)S(1)}, bf16[4,8,24,1664]{3,2,1,0:T(8,128)(2,1)}, u32[]{:S(2)}) copy-start(bf16[4,8,24,1664]{3,2,1,0:T(8,128)(2,1)} %copy-done.3) | copy-start | bytes 7667716
  215.7 8.1 %copy-start.10 = (f32[768,1024]{1,0:T(8,128)S(1)}, f32[768,1024]{1,0:T(8,128)}, u32[]{:S(2)}) copy-start(f32[768,1024]{1,0:T(8,128)} %fusion.4) | copy-start | bytes 9437188
Sparse Core Ops, SparseCore 0:
  9.6 23.0 all-gather.4
  44.7 20.8 all-gather.2
  177.8 32.3 reduce-scatter.1
where the time goes:
time: 242 us; the launch traced here: 241 us
  waiting for transfers between devices  148 us (61%)
  matrix products  36.5 us (15%)
  blocking collectives  16.9 us (7%)
  starting transfers between devices  15.7 us (6%)
  between operations  13.9 us (6%)
  local copies, waits for them, and re-layouts  10.7 us (4%)
    all_to_all x1, waiting for transfers between devices, on_device(): lax.all_to_all(send_g, 'expert', split_axis=1, concat_axis=1, tiled=True)  49.5 us
    reduce_scatter x1, waiting for transfers between devices, on_device(): lax.psum_scatter(lax.optimization_barrier(term.astype(jnp.bfloat16)).asty...  32.4 us
    all_to_all x1, waiting for transfers between devices, on_device(): lax.all_to_all(send_x, 'expert', split_axis=1, concat_axis=1, tiled=True)  30.2 us
    all_gather x1, waiting for transfers between devices, on_device(): lax.all_gather(out_grad, 'dp', axis=0, tiled=True)  17.5 us
    all_gather x1, waiting for transfers between devices, on_device(): lax.all_gather(tokens, 'dp', axis=0, tiled=True)  12.8 us
    dot_general x1, matrix products, on_device(): lax.dot_general(rows_x, d_pre, (((0,), (0,)), ((), ())), preferred_elemen...  8.06 us
    dot_general x1, matrix products, on_device(): lax.dot_general(rows_g, second_w, (((1,), (1,)), ((), ())), preferred_ele...  6.44 us
    all_gather x1, blocking collectives, on_device(): lax.all_gather(expert_index, 'dp', axis=0, tiled=True)  6.39 us
  transfers between devices with their start and end apart: 6, of which 6 were waited for; matrix products, arithmetic and copies ran while one was open for 10% of the time, Pallas kernels for 0%

commit v1 on v0

--- a/solution.py
+++ b/solution.py
@@ -67,7 +67,12 @@
     scaled_first, scaled_second = scaled(weight_all, grad_all)
     send_x, send_g = dispatch(tok_all, scaled_first, scaled_second, pick_first, pick_second)
     rows_x, rows_g = (
-        lax.all_to_all(send_x, "expert", split_axis=1, concat_axis=1, tiled=True),
+        jnp.concatenate(
+            lax.all_to_all(
+                jnp.stack(jnp.split(send_x, lax.axis_size("expert"), axis=1)), "expert", 0, 0
+            ),
+            axis=1,
+        ),
         lax.all_to_all(send_g, "expert", split_axis=1, concat_axis=1, tiled=True),
     )
     rows_x = rows_x.reshape(-1, feat_width)

time: 242 us -> 246 us (1.017)
  local copies, waits for them, and re-layouts: 10.7 us -> 15.6 us
    unnamed x24 -> x31, local copies, waits for them, and re-layouts: 3.3 us -> 9.17 us
where the time goes in v1:
time: 246 us
  waiting for transfers between devices  147 us (60%)
  matrix products  36.5 us (15%)
  blocking collectives  16.9 us (7%)
  starting transfers between devices  15.7 us (6%)
  local copies, waits for them, and re-layouts  15.6 us (6%)
  between operations  13.9 us (6%)
    all_to_all x1, waiting for transfers between devices, on_device(): lax.all_to_all(send_g, 'expert', split_axis=1, concat_axis=1, tiled=True)  49.5 us
    reduce_scatter x1, waiting for transfers between devices, on_device(): lax.psum_scatter(lax.optimization_barrier(term.astype(jnp.bfloat16)).asty...  31.8 us
    all_to_all x1, waiting for transfers between devices, on_device(): lax.all_to_all(jnp.stack(jnp.split(send_x, lax.axis_size('expert'), axis=...  30.2 us
    all_gather x1, waiting for transfers between devices, on_device(): lax.all_gather(out_grad, 'dp', axis=0, tiled=True)  17.5 us
    all_gather x1, waiting for transfers between devices, on_device(): lax.all_gather(tokens, 'dp', axis=0, tiled=True)  12.8 us
    unnamed x31, local copies, waits for them, and re-layouts  9.17 us
    dot_general x1, matrix products, on_device(): lax.dot_general(rows_x, d_pre, (((0,), (0,)), ((), ())), preferred_elemen...  8.06 us
    dot_general x1, matrix products, on_device(): lax.dot_general(rows_g, second_w, (((1,), (1,)), ((), ())), preferred_ele...  6.44 us
  transfers between devices with their start and end apart: 6, of which 6 were waited for; matrix products, arithmetic and copies ran while one was open for 10% of the time, Pallas kernels for 0%

profile of v1, /device:TPU:0, one launch (start us, length us, event | category | flops | bytes accessed | tf_op | source)
XLA Modules:
  0.0 245.7 jit_solution(1332337422130560369)
XLA Ops:
  7.2 0.0 copy-start
  7.2 0.0 all-gather.5.cloned.1.call-start
  7.2 0.7 all-gather.5.cloned.1.call-update
  7.9 6.4 %all_gather.15 = s32[512,2]{0,1:T(2,128)S(1)} all-gather(s32[128,2]{0,1:T(2,128)} %param.10), channel_id=1, replica_groups=mesh['expert'=8,'dp'=4] {'dp'}, dimensions={0}, use_global_device_ids=true | all-gather | bytes 5120 | tf_op jit(solution)/shard_map/all_gather | solution.py:61
  14.3 5.5 %all_gather.16 = s32[512,2]{0,1:T(2,128)S(1)} all-gather(s32[128,2]{0,1:T(2,128)} %param.11), channel_id=1, replica_groups=mesh['expert'=8,'dp'=4] {'dp'}, dimensions={0}, use_global_device_ids=true | all-gather | bytes 5120 | tf_op jit(solution)/shard_map/all_gather | solution.py:62
  19.9 12.8 %all-gather.5.cloned.1.call-done = bf16[512,1664]{1,0:T(8,128)(2,1)} async-done(((bf16[128,1664]{1,0:T(8,128)(2,1)}), bf16[512,1664]{1,0:T(8,128)(2,1)}) %all-gather.5.cloned.1.call-update) | async-done | bytes 1703952 | tf_op jit(solution)/shard_map/all_gather | solution.py:58
  32.7 2.3 convolution_convert_fusion
  35.0 0.7 fusion.38
  35.8 0.7 fusion.37
  36.5 0.7 fusion.36
  37.3 0.7 fusion.35
  38.0 0.7 fusion.34
  38.7 0.7 fusion.33
  39.5 0.7 fusion.32
  40.2 0.7 fusion.31
  41.0 5.6 %all-to-all-start.1 = ((bf16[8,4,1,24,1664]{4,3,1,2,0:T(8,128)(2,1)}), bf16[8,4,1,24,1664]{4,3,1,2,0:T(8,128)(2,1)}, u32[]{:S(2)}, u32[]{:S(2)}) async-start(bf16[8,4,1,24,1664]{4,3,1,2,0:T(8,128)(2,1)} %fusion.31), calls=%async_computation.1 | async-start | bytes 5111808 | tf_op jit(solution)/shard_map/all_to_all | solution.py:71
  46.6 0.0 all-gather.3.cloned.1.call-start
  46.7 0.7 all-gather.3.cloned.1.call-update
  47.4 0.0 copy-done.7
  47.4 5.0 %all_gather.17 = bf16[512,2]{0,1:T(2,128)(2,1)S(1)} all-gather(bf16[128,2]{0,1:T(2,128)(2,1)S(1)} %copy-done.7), channel_id=1, replica_groups=mesh['expert'=8,'dp'=4] {'dp'}, dimensions={0}, use_global_device_ids=true | all-gather | bytes 2560 | tf_op jit(solution)/shard_map/all_gather | solution.py:60
  52.4 17.5 %all-gather.3.cloned.1.call-done = bf16[512,1664]{1,0:T(8,128)(2,1)} async-done(((bf16[128,1664]{1,0:T(8,128)(2,1)}), bf16[512,1664]{1,0:T(8,128)(2,1)}) %all-gather.3.cloned.1.call-update) | async-done | bytes 1703952 | tf_op jit(solution)/shard_map/all_gather | solution.py:59
  69.9 2.5 %fusion.23 = f32[4,8,24,1664]{3,2,1,0:T(8,128)S(1)} fusion(bf16[4,128,1664]{2,1,0:T(8,128)(2,1)} %bitcast.131, f32[4,128]{1,0:T(4,128)S(1)} %get-tuple-element.9, pred[4,24,128]{2,1,0:T(8,128)(4,1)S(1)} %iota_compare_fusion.1, pred[4,8,128]{2,1,0:T(8,128)(4,1)S(1)} %iota_compare_fusion.3), kind=kOutput, calls=%fused_computation.29 | convolution fusion | flops 329809920 | bytes 6834176 | tf_op jit(solution)/shard_map/recn,rnd->recd/dot_general | solution.py:42
  72.4 0.0 copy-done.1
  72.4 0.9 add_convert_fusion
  73.4 1.7 copy.36
  75.0 30.2 %all-to-all-done.1 = bf16[8,4,1,24,1664]{4,3,1,2,0:T(8,128)(2,1)} async-done(((bf16[8,4,1,24,1664]{4,3,1,2,0:T(8,128)(2,1)}), bf16[8,4,1,24,1664]{4,3,1,2,0:T(8,128)(2,1)}, u32[]{:S(2)}, u32[]{:S(2)}) %all-to-all-start.1) | async-done | bytes 2555936 | tf_op jit(solution)/shard_map/all_to_all | solution.py:71
  105.2 4.4 %all-to-all-start = ((bf16[4,8,24,1664]{3,2,0,1:T(8,128)(2,1)}), bf16[4,8,24,1664]{3,2,0,1:T(8,128)(2,1)}, u32[]{:S(2)}, u32[]{:S(2)}) async-start(bf16[4,8,24,1664]{3,2,0,1:T(8,128)(2,1)} %copy.36), calls=%async_computation | async-start | bytes 5111808 | tf_op jit(solution)/shard_map/all_to_all | solution.py:76
  109.6 0.0 reduce-scatter.2.cloned.1.call-start
  109.7 1.9 copy.45
  111.6 1.5 copy-done.2
  113.1 0.0 copy-done
  113.1 4.7 %fusion.4 = f32[768,1024]{1,0:T(8,128)} fusion(bf16[768,1664]{1,0:T(8,128)(2,1)S(1)} %bitcast.134, bf16[1,1664,1024]{2,1,0:T(8,128)(2,1)S(1)} %copy-done), kind=kOutput, calls=%fused_computation.10 | convolution fusion | flops 2617245696 | bytes 9109504 | tf_op jit(solution)/shard_map/dot_general | solution.py:82
  117.8 49.5 %all-to-all-done = bf16[4,8,24,1664]{3,2,0,1:T(8,128)(2,1)} async-done(((bf16[4,8,24,1664]{3,2,0,1:T(8,128)(2,1)}), bf16[4,8,24,1664]{3,2,0,1:T(8,128)(2,1)}, u32[]{:S(2)}, u32[]{:S(2)}) %all-to-all-start) | async-done | bytes 2555936 | tf_op jit(solution)/shard_map/all_to_all | solution.py:76
  167.3 2.1 copy.37
  169.4 0.6 copy-done.8
  170.0 6.4 %convert_reduce_fusion = (f32[1024]{0:T(1024)}, bf16[768,1024]{1,0:T(8,128)(2,1)S(1)}) fusion(f32[768,1024]{1,0:T(8,128)} %fusion.4, f32[1024]{0:T(1024)S(1)} %bitcast.139, bf16[768,1664]{1,0:T(8,128)(2,1)S(1)} %bitcast.136, bf16[1,1024,1664]{2,1,0:T(8,128)(2,1)S(1)} %copy-done.8), kind=kOutput, calls=%fused_computation.22 | convolution fusion | flops 2627468288 | bytes 10690560 | tf_op jit(solution)/shard_map/dot_general | solution.py:87
  176.5 1.1 copy-done.11
  177.6 4.3 %fusion.8 = bf16[768,1664]{1,0:T(8,128)(2,1)} fusion(bf16[768,1024]{1,0:T(8,128)(2,1)S(1)} %get-tuple-element.15, bf16[1,1664,1024]{2,1,0:T(8,128)(2,1)S(1)} %copy-done), kind=kOutput, calls=%fused_computation.14 | convolution fusion | flops 2618523648 | bytes 7536640 | tf_op jit(solution)/shard_map/dot_general | solution.py:95
  181.9 0.0 reduce-scatter.2.cloned.1.call-update
  182.0 0.7 copy-done.5
  182.6 0.0 copy-done.6
  182.7 31.8 %reduce-scatter.2.cloned.1.call-done = bf16[192,1664]{1,0:T(8,128)(2,1)} async-done(((bf16[768,1664]{1,0:T(8,128)(2,1)}), bf16[192,1664]{1,0:T(8,128)(2,1)}) %reduce-scatter.2.cloned.1.call-update) | async-done | bytes 638992 | tf_op jit(solution)/shard_map/reduce_scatter | solution.py:98
  214.5 5.5 %all-to-all-start.2 = ((bf16[8,24,1664]{2,1,0:T(8,128)(2,1)}), bf16[8,24,1664]{2,1,0:T(8,128)(2,1)}, u32[]{:S(2)}, u32[]{:S(2)}) async-start(bf16[8,24,1664]{2,1,0:T(8,128)(2,1)} %bitcast.138), calls=%async_computation.3 | async-start | bytes 1277952 | tf_op jit(solution)/shard_map/all_to_all | solution.py:107
  220.0 0.0 copy-start.10
  220.0 8.1 %convolution_bitcast_fusion.1 = f32[1,1664,1024]{2,1,0:T(8,128)} fusion(bf16[768,1664]{1,0:T(8,128)(2,1)} %bitcast.135, bf16[768,1024]{1,0:T(8,128)(2,1)} %copy-done.11), kind=kOutput, calls=%fused_computation.3 | convolution fusion | flops 2617245696 | bytes 10944512 | tf_op jit(solution)/shard_map/dot_general | solution.py:92
  228.1 5.1 %convolution_bitcast_fusion = f32[1,1024,1664]{2,1,0:T(8,128)} fusion(bf16[768,1664]{1,0:T(8,128)(2,1)S(1)} %bitcast.137, f32[768,1024]{1,0:T(8,128)S(1)} %copy-done.10, f32[1024]{0:T(1024)S(1)} %bitcast.140), kind=kOutput, calls=%fused_computation.2 | convolution fusion | flops 2621964288 | bytes 12521472 | tf_op jit(solution)/shard_map/dot_general | solution.py:84
  233.2 3.9 %all-to-all-done.2 = bf16[8,24,1664]{2,1,0:T(8,128)(2,1)} async-done(((bf16[8,24,1664]{2,1,0:T(8,128)(2,1)}), bf16[8,24,1664]{2,1,0:T(8,128)(2,1)}, u32[]{:S(2)}, u32[]{:S(2)}) %all-to-all-start.2) | async-done | bytes 639008 | tf_op jit(solution)/shard_map/all_to_all | solution.py:107
  237.0 2.2 fusion.17
  (28 shorter events, 0.1 us)
Async XLA Ops:
  7.2 105.9 %copy-start = (bf16[1,1664,1024]{2,1,0:T(8,128)(2,1)S(1)}, bf16[1,1664,1024]{2,1,0:T(8,128)(2,1)}, u32[]{:S(2)}) copy-start(bf16[1,1664,1024]{2,1,0:T(8,128)(2,1)} %param.13) | copy-start | bytes 10223620
  7.2 25.5 %all-gather.5.cloned.1.call-start = ((), (), s32[]{:S(2)}) async-start(), calls=%async_computation.5 | async-start | bytes 2129920 | tf_op jit(solution)/shard_map/all_gather | solution.py:58
  41.0 6.4 %copy-start.7 = (bf16[128,2]{0,1:T(2,128)(2,1)S(1)}, bf16[128,2]{0,1:T(2,128)(2,1)}, u32[]{:S(2)}) copy-start(bf16[128,2]{0,1:T(2,128)(2,1)} %param.12) | copy-start | bytes 1540
  41.0 64.2 %all-to-all-start.1 = ((bf16[8,4,1,24,1664]{4,3,1,2,0:T(8,128)(2,1)}), bf16[8,4,1,24,1664]{4,3,1,2,0:T(8,128)(2,1)}, u32[]{:S(2)}, u32[]{:S(2)}) async-start(bf16[8,4,1,24,1664]{4,3,1,2,0:T(8,128)(2,1)} %fusion.31), calls=%async_computation.1 | async-start | bytes 5111808 | tf_op jit(solution)/shard_map/all_to_all | solution.py:71
  46.6 23.3 %all-gather.3.cloned.1.call-start = ((), (), s32[]{:S(2)}) async-start(), calls=%async_computation.4 | async-start | bytes 2129920 | tf_op jit(solution)/shard_map/all_gather | solution.py:59
  69.9 2.5 %copy-start.1 = (bf16[512,1664]{1,0:T(8,128)(2,1)S(1)}, bf16[512,1664]{1,0:T(8,128)(2,1)}, u32[]{:S(2)}) copy-start(bf16[512,1664]{1,0:T(8,128)(2,1)} %all-gather.3.cloned.1.call-done) | copy-start | bytes 5111812
  105.2 62.1 %all-to-all-start = ((bf16[4,8,24,1664]{3,2,0,1:T(8,128)(2,1)}), bf16[4,8,24,1664]{3,2,0,1:T(8,128)(2,1)}, u32[]{:S(2)}, u32[]{:S(2)}) async-start(bf16[4,8,24,1664]{3,2,0,1:T(8,128)(2,1)} %copy.36), calls=%async_computation | async-start | bytes 5111808 | tf_op jit(solution)/shard_map/all_to_all | solution.py:76
  109.6 104.8 %reduce-scatter.2.cloned.1.call-start = ((), (), s32[]{:S(2)}) async-start(), calls=%async_computation.6 | async-start | bytes 3194880 | tf_op jit(solution)/shard_map/reduce_scatter | solution.py:98
  111.6 1.5 copy-start.2
  117.8 51.6 %copy-start.9 = (f32[1,1024]{1,0:T(1,128)S(1)}, f32[1,1024]{1,0:T(1,128)}, u32[]{:S(2)}) copy-start(f32[1,1024]{1,0:T(1,128)} %param.14) | copy-start | bytes 12292
  167.3 2.7 %copy-start.8 = (bf16[1,1024,1664]{2,1,0:T(8,128)(2,1)S(1)}, bf16[1,1024,1664]{2,1,0:T(8,128)(2,1)}, u32[]{:S(2)}) copy-start(bf16[1,1024,1664]{2,1,0:T(8,128)(2,1)} %param.15) | copy-start | bytes 10223620
  169.4 7.1 %copy-start.3 = (bf16[4,8,24,1664]{3,2,1,0:T(8,128)(2,1)}, bf16[4,8,24,1664]{3,2,1,0:T(8,128)(2,1)S(1)}, u32[]{:S(2)}) copy-start(bf16[4,8,24,1664]{3,2,1,0:T(8,128)(2,1)S(1)} %copy.37) | copy-start | bytes 7667716
  176.5 1.2 copy-start.11
  181.9 0.7 copy-start.5
  181.9 0.7 copy-start.6
  214.5 22.6 %all-to-all-start.2 = ((bf16[8,24,1664]{2,1,0:T(8,128)(2,1)}), bf16[8,24,1664]{2,1,0:T(8,128)(2,1)}, u32[]{:S(2)}, u32[]{:S(2)}) async-start(bf16[8,24,1664]{2,1,0:T(8,128)(2,1)} %bitcast.138), calls=%async_computation.3 | async-start | bytes 1277952 | tf_op jit(solution)/shard_map/all_to_all | solution.py:107
  220.0 8.1 %copy-start.4 = (bf16[4,8,24,1664]{3,2,1,0:T(8,128)(2,1)S(1)}, bf16[4,8,24,1664]{3,2,1,0:T(8,128)(2,1)}, u32[]{:S(2)}) copy-start(bf16[4,8,24,1664]{3,2,1,0:T(8,128)(2,1)} %copy-done.3) | copy-start | bytes 7667716
  220.0 8.1 %copy-start.10 = (f32[768,1024]{1,0:T(8,128)S(1)}, f32[768,1024]{1,0:T(8,128)}, u32[]{:S(2)}) copy-start(f32[768,1024]{1,0:T(8,128)} %fusion.4) | copy-start | bytes 9437188
Sparse Core Ops, SparseCore 0:
  9.6 23.0 all-gather.4
  49.0 20.8 all-gather.2
  182.1 32.3 reduce-scatter.1
